TPU v7x, 256 devices: a whole 4x4x8 slice. The times are simulated.
256 devices in a mesh: prow: 8 (over z), pcol: 32 (over x, y, core).
Axes of the slice: x: 4, y: 4, z: 8, core: 2. Of those that a mesh axis runs over, the one named last changes fastest.
Arguments:
- inverse_tiles: float32 [8192, 8192], P('pcol', 'prow'), may hold values from -6 to 6
- factor: float32 [2, 8192, 512], P(None, ('pcol', 'prow')), may hold values from -0.09375 to 0.09375
- link_factor: float32 [1, 512, 512], replicated, may hold values from -0.25 to 0.25
- diag_inverse: float32 [2, 512, 512], replicated, may hold values from -3 to 3
- ancestors: int32 [2, 8], replicated, may hold values from 0 to 15, as said below
Outputs:
- offdiag: float32 [2, 8192, 512], P(None, ('pcol', 'prow'))
- diag: float32 [2, 512, 512], P(None, 'pcol')
- link_blocks: float32 [1, 512, 512], P(None, 'pcol')
Inputs may be any that keep to these rules, and one draw needn't show every extreme that they name: `ancestors`: row k lists 8 distinct stored block rows; every row lists block 15, and row 0 lists block 0.
All inputs are finite; a program needn't handle non-finite values.
Results may differ from a plain program's by a relative error of at most 0.0001.
Values sent between devices are 32-bit elements; how exact they have to be, the bound alone decides.
A program may use at most 64 MiB of HBM per device.

v0:
```python
import jax
import jax.numpy as jnp
from jax import lax
from jax.sharding import PartitionSpec as P


def broadcast(value, axis, source):
    kept = jnp.where(lax.axis_index(axis) == source, value, 0).astype(value.dtype)
    return lax.psum(kept, axis)


def product(left_part, right_part):
    return jnp.dot(
        left_part, right_part, precision=lax.Precision.HIGHEST, preferred_element_type=jnp.float32
    )


def gather_columns(row_factor, ratio, prow_index, concat_dim):
    pieces = []
    for member in range(ratio):
        pieces.append(broadcast(row_factor, "pcol", prow_index * ratio + member))
    return jnp.concatenate(pieces, axis=concat_dim)


def body(inverse_tiles, factor, link_factor, diag_inverse, ancestors):
    row_count, col_count = inverse_tiles.shape
    nsuper, unit_rows, columns = factor.shape
    prow_count = lax.axis_size("prow")
    pcol_count = lax.axis_size("pcol")
    ratio = col_count // row_count
    prow_index = lax.axis_index("prow")
    pcol_index = lax.axis_index("pcol")
    first_row = (pcol_index * prow_count + prow_index) * unit_rows
    block_ids = (first_row + lax.iota(jnp.int32, unit_rows)) // columns
    selected = jnp.any(block_ids[None, :, None] == ancestors[:, None, :], axis=2).astype(
        jnp.float32
    )
    unit_factor = factor * selected[:, :, None]
    slice_rows = columns // pcol_count
    slice_start = pcol_index * slice_rows
    offdiag_list = []
    diag_list = []
    link_list = []
    prior_offdiag = None
    prior_diag = None
    for number in range(nsuper):
        row_factor = lax.all_gather(unit_factor[number], "prow", axis=0, tiled=True)
        col_factor = gather_columns(row_factor, ratio, prow_index, 0)

        def partial_term(begin_row, row_total, col_factor=col_factor):
            return product(inverse_tiles, col_factor)

        summed = lax.psum_scatter(
            partial_term(jnp.int32(0), lax.axis_size("prow") * unit_rows),
            "prow",
            scatter_dimension=0,
            tiled=True,
        )
        local_factor = unit_factor[number]
        gram_part = product(local_factor.T, summed)
        keep_rows = selected[number][:, None]
        if number == 0:
            gram_sum = lax.psum(gram_part, ("prow", "pcol"))
            result = -(keep_rows * summed)
            diag_block = diag_inverse[0] + gram_sum
        else:
            link_block = link_factor[number - 1]
            cross_part = product(prior_offdiag.T, local_factor)
            gram_sum, cross_sum = lax.psum((gram_part, cross_part), ("prow", "pcol"))
            result = -(keep_rows * (summed + product(prior_offdiag, link_block)))
            link_out = -(cross_sum + product(prior_diag, link_block))
            diag_block = (
                diag_inverse[number]
                + gram_sum
                + product(cross_sum.T, link_block)
                - product(link_block.T, link_out)
            )
            link_list.append(lax.dynamic_slice_in_dim(link_out, slice_start, slice_rows, 0))
        offdiag_list.append(result)
        diag_list.append(lax.dynamic_slice_in_dim(diag_block, slice_start, slice_rows, 0))
        prior_offdiag = result
        prior_diag = diag_block
    return (jnp.stack(offdiag_list), jnp.stack(diag_list), jnp.stack(link_list))


def solution(mesh):
    in_specs = (P("pcol", "prow"), P(None, ("pcol", "prow"), None), P(), P(), P())
    out_specs = (P(None, ("pcol", "prow"), None), P(None, "pcol", None), P(None, "pcol", None))
    return jax.shard_map(body, mesh=mesh, in_specs=in_specs, out_specs=out_specs, check_vma=False)
```

profile of v0, /device:TPU:1, one launch (start us, length us, event | category | flops | bytes accessed | tf_op | source)
XLA Modules:
  0.0 557.4 jit_solution(3136330771844192)
XLA Ops:
  7.3 0.8 compare_reduce_fusion
  8.1 1.0 broadcast_multiply_fusion
  9.1 23.7 %all-gather = f32[1,256,512]{2,1,0:T(8,128)S(1)} all-gather(f32[1,32,512]{2,1,0:T(8,128)S(1)} %get-tuple-element.25), channel_id=2, replica_groups=mesh['prow'=8,'pcol'=32] {'prow'}, dimensions={1}, use_global_device_ids=true | all-gather | bytes 589824 | tf_op jit(solution)/shard_map/all_gather | solution.py:47
  32.8 19.3 %all-gather.1 = f32[1,256,512]{2,1,0:T(8,128)S(1)} all-gather(f32[1,32,512]{2,1,0:T(8,128)S(1)} %get-tuple-element.26), channel_id=3, replica_groups=mesh['prow'=8,'pcol'=32] {'prow'}, dimensions={1}, use_global_device_ids=true | all-gather | bytes 589824 | tf_op jit(solution)/shard_map/all_gather | solution.py:47
  52.2 1.4 select_bitcast_fusion.7
  53.6 1.4 select_bitcast_fusion.3
  55.1 0.0 reduce-scatter.7.cloned.1.call-start
  55.1 134.1 %all-reduce.7.cloned.1.call-done = (f32[256,512]{1,0:T(8,128)}, f32[256,512]{1,0:T(8,128)}, f32[256,512]{1,0:T(8,128)}, f32[256,512]{1,0:T(8,128)}, f32[256,512]...) async-done(((f32[256,512]{1,0:T(8,128)}, f32[256,512]{1,0:T(8,128)}, f32[256,512]{1,0:T(8,128)}, f32[256,512]{1,0:T(8,128)}, ...) | async-done | bytes 4194320 | tf_op jit(solution)/shard_map/psum | solution.py:9
  189.2 5.0 fusion.20
  194.2 1.0 copy.14
  195.2 0.0 reduce-scatter.9.cloned.1.call-start
  195.3 4.8 fusion.17
  200.1 1.0 copy.16
  201.2 0.2 all-reduce.5.cloned.1.call-start
  201.4 26.6 %reduce-scatter.7.cloned.1.call-done = f32[32,512]{1,0:T(8,128)} async-done(((f32[256,512]{1,0:T(8,128)}), f32[32,512]{1,0:T(8,128)}) %reduce-scatter.7.cloned.1.call-update) | async-done | bytes 65552
  228.0 1.0 copy.15
  229.0 2.8 fusion.38
  231.8 2.0 fusion.31
  233.8 33.1 %reduce-scatter.9.cloned.1.call-done = f32[32,512]{1,0:T(8,128)} async-done(((f32[256,512]{1,0:T(8,128)}), f32[32,512]{1,0:T(8,128)}) %reduce-scatter.9.cloned.1.call-update) | async-done | bytes 65552
  266.9 2.9 fusion.35
  269.8 1.1 slice_bitcast_fusion
  270.9 0.7 fusion.32
  271.6 1.0 copy.13
  272.6 0.7 fusion.25
  273.3 0.7 pad_maximum_fusion
  274.0 267.6 %all-reduce.5.cloned.1.call-done = (f32[512,512]{1,0:T(8,128)}, f32[512,512]{1,0:T(8,128)}, f32[512,512]{1,0:T(8,128)}) async-done(((f32[512,512]{1,0:T(8,128)}, f32[512,512]{1,0:T(8,128)}, f32[512,512]{1,0:T(8,128)}), (f32[512,512]{1,0:T(8,128)}, f32[512,512]{1,0:T(8,128)}, f32[512,512]{1,0:T(8,128)})) %all-reduce.5.cloned.1.call-update) | async-done | bytes 3145744 | tf_op jit(solution)/shard_map/psum | solution.py:69
  541.7 1.5 bitcast_add_fusion
  543.2 1.9 fusion.28
  545.1 1.9 fusion.16
  546.9 1.9 convolution_bitcast_fusion
  548.8 1.4 fusion.40
  550.2 0.6 pad_maximum_fusion.1
  (22 shorter events, 0.2 us)
Async XLA Ops:
  7.2 265.5 %copy-start = (f32[1,512,512]{2,1,0:T(8,128)S(1)}, f32[1,512,512]{2,1,0:T(8,128)}, u32[]{:S(2)}) copy-start(f32[1,512,512]{2,1,0:T(8,128)} %param.7) | copy-start | bytes 3145732
  7.2 182.0 %all-reduce.7.cloned.1.call-start = ((), (), s32[]{:S(2)}) async-start(), calls=%async_computation.5 | async-start | bytes 8388608 | tf_op jit(solution)/shard_map/psum | solution.py:9
  55.0 134.1 %copy-start.4 = (f32[256,1024]{1,0:T(8,128)S(1)}, f32[256,1024]{1,0:T(8,128)}, u32[]{:S(2)}) copy-start(f32[256,1024]{1,0:T(8,128)} %param.5) | copy-start | bytes 3145732
  55.1 173.0 %reduce-scatter.7.cloned.1.call-start = ((), (), s32[]{:S(2)}) async-start(), calls=%async_computation.2 | async-start | bytes 589824
  189.2 6.1 %copy-start.5 = (f32[256,512]{1,0:T(8,128)S(1)}, f32[256,512]{1,0:T(8,128)}, u32[]{:S(2)}) copy-start(f32[256,512]{1,0:T(8,128)} %get-tuple-element.9) | copy-start | bytes 1572868
  195.2 71.7 %reduce-scatter.9.cloned.1.call-start = ((), (), s32[]{:S(2)}) async-start(), calls=%async_computation.3 | async-start | bytes 589824
  201.2 340.5 %all-reduce.5.cloned.1.call-start = ((), (), s32[]{:S(2)}) async-start(), calls=%async_computation.4 | async-start | bytes 6291456 | tf_op jit(solution)/shard_map/psum | solution.py:69
  233.8 36.0 %copy-start.2 = (f32[2,512,512]{2,1,0:T(8,128)S(1)}, f32[2,512,512]{2,1,0:T(8,128)}, u32[]{:S(2)}) copy-start(f32[2,512,512]{2,1,0:T(8,128)} %param.8) | copy-start | bytes 6291460
  269.8 2.8 copy-start.3
  541.7 1.5 copy-start.1
Sparse Core Ops, SparseCore 0:
  55.2 133.9 all-reduce.6
  195.4 32.6 reduce-scatter.6
  230.5 36.3 reduce-scatter.8
  272.5 269.0 all-reduce.4
where the time goes:
time: 558 us; the launch traced here: 557 us
  waiting for transfers between devices  461 us (83%)
  blocking collectives  43.1 us (8%)
  matrix products  23.8 us (4%)
  between operations  13.9 us (2%)
  other arithmetic  9.63 us (2%)
    psum x1, waiting for transfers between devices, body(): gram_sum, cross_sum = lax.psum((gram_part, cross_part), ('prow', 'pcol'))  268 us
    psum x1, waiting for transfers between devices, broadcast(): return lax.psum(kept, axis)  134 us
    unnamed x6, waiting for transfers between devices  59.8 us
    all_gather x2, blocking collectives, body(): row_factor = lax.all_gather(unit_factor[number], 'prow', axis=0, tiled=True)  43.1 us
    dot_general x9, matrix products, product(): jnp.dot(left_part, right_part, precision=lax.Precision.HIGHEST, preferred...  23.8 us
  transfers between devices with their start and end apart: 4, of which 4 were waited for; matrix products, arithmetic and copies ran while one was open for 3% of the time, Pallas kernels for 0%

commit v1 on v0

v1 whole, which is shorter than its diff:
```python
import functools

import jax
import jax.numpy as jnp
from jax import lax
from jax.experimental import pallas as pl
from jax.experimental.pallas import tpu as pltpu
from jax.sharding import PartitionSpec as P

MESH = pl.DeviceIdType.MESH
F32 = jnp.float32
BF16 = jnp.bfloat16
CHUNKS = 4


def split(value):
    high = value.astype(BF16)
    low = (value - high.astype(F32)).astype(BF16)
    return high, low


def dot(left, right):
    return jnp.dot(left, right, preferred_element_type=F32)


def dot3(left, right):
    left_high, left_low = left
    right_high, right_low = right
    return dot(left_high, right_high) + dot(left_high, right_low) + dot(left_low, right_high)


def kernel(
    tiles_hbm, factor_ref, link_hbm, dinv_hbm, anc_ref,
    off_ref, diag_ref, link_ref,
    tiles_v, tiles_hi, tiles_lo, first, factor_z, factor_split, part, arrive, rows, pair_factor,
    link_v, link_hi, link_lo, dinv0_v, dinv1_v, extra,
    left_buf, right_buf, gram, gram_in, line, line_in, plane, z_in, total, final,
    local_sem, first_sem, spread_sem, pair_sem, one_sem, two_sem, ring_sem, rows_sem,
    gram_sem, line_sem, z_sem, final_sem, send_sem, group_send,
):
    z = lax.axis_index("prow")
    p = lax.axis_index("pcol")
    core = lax.rem(p, 2)
    x = p // 8
    y = lax.rem(p // 2, 4)
    a = x + core * (y - x)
    b = y + core * (x - y)
    block = p // 2

    def device(dest_z, dest_a, dest_b):
        dest_x = dest_a + core * (dest_b - dest_a)
        dest_y = dest_b + core * (dest_a - dest_b)
        return (dest_z, (dest_x * 4 + dest_y) * 2 + core)

    def local(src, dst, sem):
        copy = pltpu.make_async_copy(src, dst, sem)
        copy.start()
        return copy

    sent = []

    def send(src, dst, recv, target):
        copy = pltpu.make_async_remote_copy(
            src_ref=src, dst_ref=dst, send_sem=send_sem.at[len(sent)], recv_sem=recv,
            device_id=target, device_id_type=MESH,
        )
        copy.start()
        sent.append(copy)

    def send_group(src, dst, recv, target, group):
        pltpu.make_async_remote_copy(
            src_ref=src, dst_ref=dst, send_sem=group_send.at[group], recv_sem=recv,
            device_id=target, device_id_type=MESH,
        ).start()

    def wait_bytes(ref, sem):
        pltpu.make_async_copy(ref, ref, sem).wait()

    own_tiles = local(tiles_hbm, tiles_v.at[core], local_sem.at[0])
    own_link = local(link_hbm.at[0], link_v, local_sem.at[1])
    own_dinv0 = local(dinv_hbm.at[0], dinv0_v, local_sem.at[2])
    slice_rows = pl.ds(pl.multiple_of(p * 16, 16), 16)
    own_dinv1 = local(dinv_hbm.at[:, slice_rows], dinv1_v, local_sem.at[3])

    barrier = pltpu.get_barrier_semaphore()
    for step in range(1, 32):
        pl.semaphore_signal(barrier, inc=1, device_id=(z, lax.rem(p + step, 32)), device_id_type=MESH)
    for step in range(1, 8):
        for other in range(2):
            pl.semaphore_signal(
                barrier, inc=1, device_id=(lax.rem(z + step, 8), (p // 2) * 2 + other), device_id_type=MESH
            )
    pl.semaphore_wait(barrier, 31 + 14)

    partner = (z, p + 1 - 2 * core)

    def tile_of(target):
        number = lax.rem(target, 2)
        tx = target // 8
        ty = lax.rem(target // 2, 4)
        lane = tx + number * (ty - tx)
        row = ty + number * (tx - ty)
        return factor_ref.at[
            number, pl.ds(pl.multiple_of(row * 8, 8), 8), pl.ds(pl.multiple_of(lane * 128, 128), 128)
        ]

    for step in range(1, 32):
        target = lax.rem(p + step, 32)
        send_group(tile_of(target), first.at[p], first_sem, (z, target), 0)
    local(tile_of(p), first.at[p], first_sem)

    send(tiles_hbm, tiles_v.at[core], pair_sem.at[0], partner)
    send(factor_ref, pair_factor.at[core], pair_sem.at[1], partner)
    own_pair = local(factor_ref, pair_factor.at[core], local_sem.at[4])

    wait_bytes(first, first_sem)
    mine = factor_z.at[a, :, z, b]
    for step in range(1, 8):
        dest_z = lax.rem(z + step, 8)
        send_group(first.at[pl.ds(4 * dest_z, 4)], mine, spread_sem, (dest_z, p), 1)
    local(first.at[pl.ds(4 * z, 4)], mine, spread_sem)

    def keep_of(number, row_block):
        listed = anc_ref[number, 0] == row_block
        for entry in range(1, anc_ref.shape[1]):
            listed = jnp.logical_or(listed, anc_ref[number, entry] == row_block)
        return jnp.where(listed, jnp.float32(1), jnp.float32(0))

    keep_low = keep_of(core, 2 * z)
    keep_high = keep_of(core, 2 * z + 1)
    keep0 = keep_of(0, block)
    keep1 = keep_of(1, block)

    own_tiles.wait()

    def split_tiles(half):
        def go(step, carry):
            at = pl.ds(pl.multiple_of(step * 32, 32), 32)
            high, low = split(tiles_v[half, at, :])
            put = pl.ds(pl.multiple_of(half * 256 + step * 32, 32), 32)
            tiles_hi[put, :] = high
            tiles_lo[put, :] = low
            return carry

        lax.fori_loop(0, 8, go, 0)

    split_tiles(core)
    own_link.wait()
    own_dinv0.wait()
    own_dinv1.wait()

    def split_link(step, carry):
        at = pl.ds(pl.multiple_of(step * 32, 32), 32)
        high, low = split(link_v[at, :])
        link_hi[at, :] = high
        link_lo[at, :] = low
        return carry

    lax.fori_loop(0, 16, split_link, 0)

    sent[0].wait_recv()
    split_tiles(1 - core)

    def piece(lane, row):
        return factor_z.at[lane, :, :, row]

    def half(lane, row, which):
        return factor_z.at[lane, pl.ds(2 * which, 2), :, row]

    a_next, a_prev, a_far = lax.rem(a + 1, 4), lax.rem(a + 3, 4), lax.rem(a + 2, 4)
    b_next, b_prev, b_far = lax.rem(b + 1, 4), lax.rem(b + 3, 4), lax.rem(b + 2, 4)
    to_b_next, to_b_prev = device(z, a, b_next), device(z, a, b_prev)
    to_a_next, to_a_prev = device(z, a_next, b), device(z, a_prev, b)

    def along_a(row, order):
        send(piece(a, row), piece(a, row), two_sem.at[0, order], to_a_next)
        send(piece(a, row), piece(a, row), two_sem.at[1, order], to_a_prev)

    wait_bytes(piece(a, b), spread_sem)
    send(piece(a, b), piece(a, b), one_sem.at[0], to_b_next)
    send(piece(a, b), piece(a, b), one_sem.at[1], to_b_prev)
    along_a(b, 0)

    row_ids = lax.broadcasted_iota(jnp.int32, (16, 512), 0) + p * 16
    col_ids = lax.broadcasted_iota(jnp.int32, (16, 512), 1)
    pick = jnp.where(row_ids == col_ids, jnp.float32(1), jnp.float32(0)).astype(BF16)
    across = (((1,), (1,)), ((), ()))
    picked = lax.dot_general(pick, link_hi[...], across, preferred_element_type=F32) + lax.dot_general(
        pick, link_lo[...], across, preferred_element_type=F32
    )
    picked = dot3(split(picked), split(dinv0_v[...]))
    extra[...] = dot3(split(picked), (link_hi[...], link_lo[...]))

    wait_bytes(piece(a, b_prev), one_sem.at[0])
    send(half(a, b_prev, 0), half(a, b_prev, 0), one_sem.at[2], to_b_next)
    along_a(b_prev, 1)
    wait_bytes(piece(a, b_next), one_sem.at[1])
    send(half(a, b_next, 1), half(a, b_next, 1), one_sem.at[3], to_b_prev)
    along_a(b_next, 2)
    wait_bytes(half(a, b_far, 0), one_sem.at[2])
    wait_bytes(half(a, b_far, 1), one_sem.at[3])
    along_a(b_far, 3)
    row_order = (b, b_prev, b_next, b_far)

    def relay(order):
        row = row_order[order]
        wait_bytes(piece(a_prev, row), two_sem.at[0, order])
        send(half(a_prev, row, 0), half(a_prev, row, 0), two_sem.at[2, order], to_a_next)
        wait_bytes(piece(a_next, row), two_sem.at[1, order])
        send(half(a_next, row, 1), half(a_next, row, 1), two_sem.at[3, order], to_a_prev)

    def compute(number, lane):
        def prepare(step, carry):
            value = factor_z[lane, step].reshape(256, 128)
            value = value * jnp.where(step < 2, keep_low, keep_high)
            high, low = split(value)
            at = pl.ds(pl.multiple_of(step * 256, 256), 256)
            factor_split[at, 0:128] = high
            factor_split[at, 128:256] = low
            return carry

        lax.fori_loop(0, 4, prepare, 0)

        def multiply(step, carry):
            at = pl.ds(pl.multiple_of(step * 128, 128), 128)
            both = dot(tiles_hi[at, :], factor_split[...])
            result = both[:, 0:128] + both[:, 128:256] + dot(tiles_lo[at, :], factor_split[:, 0:128])
            part[number, step // 2, pl.ds(lax.rem(step, 2) * 4, 4)] = result.reshape(4, 32, 128)
            return carry

        lax.fori_loop(0, 4, multiply, 0)

    to_z_next, to_z_prev = (lax.rem(z + 1, 8), p), (lax.rem(z + 7, 8), p)

    def hops(number):
        return (4, 3) if number % 2 == 0 else (3, 4)

    def ring(number, step):
        forward, backward = hops(number)
        if step < forward:
            dest = lax.rem(z + forward - step, 8)
            if step:
                wait_bytes(arrive.at[number, step - 1], ring_sem.at[number, step - 1])
                part[number, :, dest] = part[number, :, dest] + arrive[number, step - 1]
            send(part.at[number, :, dest], arrive.at[number, step], ring_sem.at[number, step], to_z_next)
        if step < backward:
            dest = lax.rem(z + 8 - backward + step, 8)
            slot = forward + step
            if step:
                wait_bytes(arrive.at[number, slot - 1], ring_sem.at[number, slot - 1])
                part[number, :, dest] = part[number, :, dest] + arrive[number, slot - 1]
            send(part.at[number, :, dest], arrive.at[number, slot], ring_sem.at[number, slot], to_z_prev)

    def ring_end(number, lane):
        forward, _ = hops(number)
        wait_bytes(arrive.at[number, forward - 1], ring_sem.at[number, forward - 1])
        wait_bytes(arrive.at[number, 6], ring_sem.at[number, 6])
        value = part[number, :, z] + arrive[number, forward - 1] + arrive[number, 6]
        rows[core, lane] = value.reshape(64, 128)
        send(rows.at[core, lane], rows.at[core, lane], rows_sem.at[number], partner)

    compute(0, a)
    ring(0, 0)
    relay(0)
    relay(1)
    ring(0, 1)
    relay(2)
    relay(3)
    ring(0, 2)
    compute(1, a_prev)
    ring(1, 0)
    ring(0, 3)
    compute(2, a_next)
    ring(2, 0)
    ring(1, 1)
    for order in range(4):
        wait_bytes(half(a_far, row_order[order], 0), two_sem.at[2, order])
        wait_bytes(half(a_far, row_order[order], 1), two_sem.at[3, order])
    compute(3, a_far)
    ring(3, 0)
    ring(2, 1)
    ring(1, 2)
    ring_end(0, a)
    ring(3, 1)
    ring(2, 2)
    ring(1, 3)
    ring(3, 2)
    ring(2, 3)
    ring_end(1, a_prev)
    ring(3, 3)
    ring_end(2, a_next)

    own_pair.wait()
    wait_bytes(pair_factor.at[1 - core], pair_sem.at[1])

    def own_rows(number, keep):
        return jnp.concatenate([pair_factor[0, number], pair_factor[1, number]], axis=0) * keep

    masked0 = own_rows(0, keep0)
    masked1 = own_rows(1, keep1)
    link_pair = (link_hi[...], link_lo[...])
    linked0 = dot3(split(masked0), link_pair)

    def put_left(at, value):
        high, low = split(value)
        left_buf[at:at + 64, :] = high
        left_buf[at + 64:at + 128, :] = high
        left_buf[at + 128:at + 192, :] = low

    half_cols = pl.ds(pl.multiple_of(core * 256, 256), 256)

    def put_right(at, value):
        high, low = split(value)
        right_buf[at:at + 64, :] = high
        right_buf[at + 64:at + 128, :] = low
        right_buf[at + 128:at + 192, :] = high

    put_left(0, -masked0)
    put_left(384, masked1)
    put_left(768, -linked0)

    ring_end(3, a_far)
    for number in range(CHUNKS):
        wait_bytes(rows.at[1 - core, 0], rows_sem.at[number])

    def joined(number):
        return jnp.concatenate([rows[number, lane] for lane in range(4)], axis=1)

    off0 = joined(0) * (-keep0)
    total[0] = off0
    total[3] = masked1
    put_left(192, off0)
    put_right(0, total[0, :, half_cols])
    put_right(192, total[3, :, half_cols])

    flip = (((0,), (0,)), ((), ()))

    def product(mat, first_row, row_count, right_row, swap):
        def go(step, carry):
            lanes = pl.ds(pl.multiple_of(step * 128, 128), 128)
            value = lax.dot_general(
                left_buf[first_row:first_row + row_count, lanes],
                right_buf[right_row:right_row + row_count, :],
                flip, preferred_element_type=F32,
            )
            for inner in range(4):
                upper = step + swap * (inner - step)
                lower = inner + swap * (step - inner)
                gram[mat, upper, lower] = value[inner * 32:(inner + 1) * 32, :]
            return carry

        lax.fori_loop(0, 4, go, 0)

    own_first = (a, b, a)
    own_second = (b, a, b)
    next_first = (to_a_next, to_b_next, to_a_next)
    prev_first = (to_a_prev, to_b_prev, to_a_prev)

    def gram_start(mat):
        up = lax.rem(own_first[mat] + 1, 4)
        down = lax.rem(own_first[mat] + 3, 4)
        far = lax.rem(own_first[mat] + 2, 4)
        low, high = pl.ds(0, 2), pl.ds(2, 2)
        send(gram.at[mat, far, low], gram_in.at[mat, 0], gram_sem.at[mat, 0], next_first[mat])
        send(gram.at[mat, far, high], gram_in.at[mat, 1], gram_sem.at[mat, 1], prev_first[mat])
        send(gram.at[mat, up, high], gram_in.at[mat, 2], gram_sem.at[mat, 2], next_first[mat])
        send(gram.at[mat, down, low], gram_in.at[mat, 3], gram_sem.at[mat, 3], prev_first[mat])

    def gram_middle(mat):
        up = lax.rem(own_first[mat] + 1, 4)
        down = lax.rem(own_first[mat] + 3, 4)
        low, high = pl.ds(0, 2), pl.ds(2, 2)
        wait_bytes(gram_in.at[mat, 0], gram_sem.at[mat, 0])
        gram[mat, up, low] = gram[mat, up, low] + gram_in[mat, 0]
        send(gram.at[mat, up, low], gram_in.at[mat, 4], gram_sem.at[mat, 4], next_first[mat])
        wait_bytes(gram_in.at[mat, 1], gram_sem.at[mat, 1])
        gram[mat, down, high] = gram[mat, down, high] + gram_in[mat, 1]
        send(gram.at[mat, down, high], gram_in.at[mat, 5], gram_sem.at[mat, 5], prev_first[mat])

    def gram_end(mat):
        here = own_first[mat]
        low, high = pl.ds(0, 2), pl.ds(2, 2)
        wait_bytes(gram_in.at[mat, 2], gram_sem.at[mat, 2])
        wait_bytes(gram_in.at[mat, 3], gram_sem.at[mat, 3])
        wait_bytes(gram_in.at[mat, 4], gram_sem.at[mat, 4])
        wait_bytes(gram_in.at[mat, 5], gram_sem.at[mat, 5])
        line[mat, low] = gram[mat, here, low] + gram_in[mat, 3] + gram_in[mat, 4]
        line[mat, high] = gram[mat, here, high] + gram_in[mat, 2] + gram_in[mat, 5]
        for step in range(1, 4):
            other = lax.rem(own_second[mat] + step, 4)
            target = device(z, a, other) if mat != 1 else device(z, other, b)
            send(line.at[mat, other], line_in.at[mat, step - 1], line_sem.at[mat, step - 1], target)

    def line_end(mat):
        for step in range(3):
            wait_bytes(line_in.at[mat, step], line_sem.at[mat, step])
        value = line[mat, own_second[mat]] + line_in[mat, 0] + line_in[mat, 1] + line_in[mat, 2]
        for row in range(4):
            for lane in range(2):
                plane[2 * row + lane, mat] = value[row * 8:(row + 1) * 8, lane * 128:(lane + 1) * 128]

    product(0, 0, 192, 0, core)
    gram_start(0)
    product(1, 192, 192, 192, 1 - core)
    gram_start(1)

    shifted = dot3(split(off0), link_pair)
    total[1] = shifted
    put_left(576, shifted)
    inner = joined(1) + shifted
    total[2] = inner
    put_right(384, total[2, :, half_cols])
    put_right(576, total[3, :, half_cols])
    put_right(768, total[1, :, half_cols])
    product(2, 384, 576, 384, core)
    gram_start(2)

    mine_rows = pl.ds(pl.multiple_of(core * 32, 32), 32)
    off_ref[0] = total[0, mine_rows, :]
    off_ref[1] = total[2, mine_rows, :] * (-keep1)

    for mat in range(3):
        gram_middle(mat)
    for mat in range(3):
        gram_end(mat)
    for mat in range(3):
        line_end(mat)

    for step in range(1, 8):
        dest_z = lax.rem(z + step, 8)
        send_group(plane.at[dest_z], z_in.at[z], z_sem, (dest_z, p), 2)
    local(plane.at[z], z_in.at[z], z_sem)
    wait_bytes(z_in, z_sem)
    value = z_in[0]
    for other in range(1, 8):
        value = value + z_in[other]
    plane_total = final.at[8]
    final[8] = value
    owner = z // 4
    slot = lax.rem(z, 4) * 2 + core
    for step in range(1, 8):
        send_group(plane_total, final.at[slot], final_sem, (lax.rem(z + step, 8), (p // 2) * 2 + owner), 3)

    @pl.when(owner == core)
    def _():
        local(plane_total, final.at[slot], final_sem)

    @pl.when(owner != core)
    def _():
        send_group(plane_total, final.at[slot], final_sem, partner, 4)

    wait_bytes(final.at[pl.ds(0, 8)], final_sem)

    def slice_of(mat):
        tiles = []
        for row in range(2):
            lanes = [final[(2 * row + lane) * 2 + side, mat] for side in range(2) for lane in range(2)]
            tiles.append(jnp.concatenate(lanes, axis=1))
        return jnp.concatenate(tiles, axis=0)

    diag0 = dinv1_v[0] + slice_of(0)
    diag_ref[0] = diag0
    link_ref[0] = -(slice_of(1) + dot3(split(diag0), (link_hi[...], link_lo[...])))
    diag_ref[1] = dinv1_v[1] + extra[...] + slice_of(2)

    for copy in sent:
        copy.wait_send()
    wait_bytes(first.at[pl.ds(0, 31)], group_send.at[0])
    wait_bytes(first.at[pl.ds(0, 28)], group_send.at[1])
    wait_bytes(plane.at[pl.ds(0, 7)], group_send.at[2])
    wait_bytes(plane.at[pl.ds(0, 7)], group_send.at[3])

    @pl.when(owner != core)
    def _():
        wait_bytes(plane.at[0], group_send.at[4])


def body(inverse_tiles, factor, link_factor, diag_inverse, ancestors):
    anywhere = pl.BlockSpec(memory_space=pl.ANY)
    vmem = pl.BlockSpec(memory_space=pltpu.VMEM)
    dma = pltpu.SemaphoreType.DMA
    return pl.pallas_call(
        kernel,
        out_shape=(
            jax.ShapeDtypeStruct((2, 32, 512), F32),
            jax.ShapeDtypeStruct((2, 16, 512), F32),
            jax.ShapeDtypeStruct((1, 16, 512), F32),
        ),
        in_specs=[anywhere, vmem, anywhere, anywhere, pl.BlockSpec(memory_space=pltpu.SMEM)],
        out_specs=(vmem, vmem, vmem),
        scratch_shapes=[
            pltpu.VMEM((2, 256, 1024), F32),
            pltpu.VMEM((512, 1024), BF16),
            pltpu.VMEM((512, 1024), BF16),
            pltpu.VMEM((32, 8, 128), F32),
            pltpu.VMEM((4, 4, 8, 4, 8, 128), F32),
            pltpu.VMEM((1024, 256), BF16),
            pltpu.VMEM((CHUNKS, 2, 8, 32, 128), F32),
            pltpu.VMEM((CHUNKS, 7, 2, 32, 128), F32),
            pltpu.VMEM((2, 4, 64, 128), F32),
            pltpu.VMEM((2, 2, 32, 512), F32),
            pltpu.VMEM((512, 512), F32),
            pltpu.VMEM((512, 512), BF16),
            pltpu.VMEM((512, 512), BF16),
            pltpu.VMEM((512, 512), F32),
            pltpu.VMEM((2, 16, 512), F32),
            pltpu.VMEM((16, 512), F32),
            pltpu.VMEM((960, 512), BF16),
            pltpu.VMEM((960, 256), BF16),
            pltpu.VMEM((3, 4, 4, 32, 256), F32),
            pltpu.VMEM((3, 6, 2, 32, 256), F32),
            pltpu.VMEM((3, 4, 32, 256), F32),
            pltpu.VMEM((3, 3, 32, 256), F32),
            pltpu.VMEM((8, 3, 8, 128), F32),
            pltpu.VMEM((8, 3, 8, 128), F32),
            pltpu.VMEM((4, 64, 512), F32),
            pltpu.VMEM((9, 3, 8, 128), F32),
            dma((5,)),
            dma,
            dma,
            dma((2,)),
            dma((4,)),
            dma((4, 4)),
            dma((CHUNKS, 7)),
            dma((CHUNKS,)),
            dma((3, 6)),
            dma((3, 3)),
            dma,
            dma,
            dma((96,)),
            dma((5,)),
        ],
        compiler_params=pltpu.CompilerParams(
            collective_id=0, has_side_effects=True, vmem_limit_bytes=48 * 1024 * 1024
        ),
    )(inverse_tiles, factor, link_factor, diag_inverse, ancestors)


def solution(mesh):
    in_specs = (P("pcol", "prow"), P(None, ("pcol", "prow"), None), P(), P(), P())
    out_specs = (P(None, ("pcol", "prow"), None), P(None, "pcol", None), P(None, "pcol", None))
    return jax.shard_map(body, mesh=mesh, in_specs=in_specs, out_specs=out_specs, check_vma=False)
```

time: 558 us -> 95.8 us (0.17)
  waiting for transfers between devices: 461 us -> 0 us
  Pallas kernels: 0 us -> 87.4 us
  blocking collectives: 43.1 us -> 0 us
  matrix products: 23.8 us -> 0 us
  between operations: 13.9 us -> 0.65 us
  other arithmetic: 9.63 us -> 0 us
    psum x2 -> x0, waiting for transfers between devices: 402 us -> none  [the longest x1 268 us: body(): gram_sum, cross_sum = lax.psum((gram_part, cross_part), ('prow', 'pcol'))]
    pallas_call x0 -> x1, Pallas kernels: none -> 87.4 us  [body(): pl.pallas_call(kernel, out_shape=(jax.ShapeDtypeStruct((2, 32, 512), F32)...]
    unnamed x6 -> x0, waiting for transfers between devices: 59.8 us -> none
    all_gather x2 -> x0, blocking collectives: 43.1 us -> none  [body(): row_factor = lax.all_gather(unit_factor[number], 'prow', axis=0, tiled=True)]
    dot_general x9 -> x0, matrix products: 23.8 us -> none  [product(): jnp.dot(left_part, right_part, precision=lax.Precision.HIGHEST, preferred...]
  transfers between devices with their start and end apart: 4 -> 0, of which waited for: 4 -> 0; matrix products, arithmetic and copies ran while one was open for 3% -> 0% of each run, Pallas kernels for 0% -> 0%
where the time goes in v1:
time: 95.8 us; the launch traced here: 95.6 us
  Pallas kernels  87.4 us (91%)
  local copies, waits for them, and re-layouts  7.52 us (8%)
    pallas_call x1, Pallas kernels, body(): pl.pallas_call(kernel, out_shape=(jax.ShapeDtypeStruct((2, 32, 512), F32)...  87.4 us
    unnamed x13, local copies, waits for them, and re-layouts  7.52 us

profile of v1, /device:TPU:1, one launch (start us, length us, event | category | flops | bytes accessed | tf_op | source)
XLA Modules:
  0.0 95.6 jit_solution(17530656671468326983)
XLA Ops:
  0.6 0.0 copy-start
  0.6 1.6 %copy-done = f32[2,512,512]{2,1,0:T(8,128)S(1)} copy-done((f32[2,512,512]{2,1,0:T(8,128)S(1)}, f32[2,512,512]{2,1,0:T(8,128)}, u32[]{:S(2)}) %copy-start) | copy-done | bytes 2097176
  2.2 0.0 copy-start.1
  2.2 1.2 %copy-done.1 = f32[256,1024]{1,0:T(8,128)S(1)} copy-done((f32[256,1024]{1,0:T(8,128)S(1)}, f32[256,1024]{1,0:T(8,128)}, u32[]{:S(2)}) %copy-start.1) | copy-done | bytes 1048600
  3.4 0.0 copy-start.2
  3.5 1.2 %copy-done.2 = f32[1,512,512]{2,1,0:T(8,128)S(1)} copy-done((f32[1,512,512]{2,1,0:T(8,128)S(1)}, f32[1,512,512]{2,1,0:T(8,128)}, u32[]{:S(2)}) %copy-start.2) | copy-done | bytes 1048600
  4.7 0.0 copy-start.3
  4.7 0.9 copy-done.3
  5.6 0.0 copy-start.4
  5.6 0.7 copy-done.4
  6.3 87.4 %shard_map.76 = (f32[2,32,512]{2,1,0:T(8,128)S(1)}, f32[2,16,512]{2,1,0:T(8,128)S(1)}, f32[1,16,512]{2,1,0:T(8,128)S(1)}) custom-call(f32[256,1024]{1,0:T(8,128)S(1)} %copy-done.1, f32[2,32,512]{2,1,0:T(8,128)S(1)} %copy-done.3, f32[1,512,512]{2,1,0:T(8,128)S(1)} %copy-done.2, f32[2,512,512]{2,1,0:T(8,128)S(1)} %copy-done, s32[2,8]{1,0:T(2,128)S(1)} %copy-done.4), custom_call_target="tpu_custom_call" | custom-call | tf_op jit(solution)/shard_map/pallas_call | solution.py:482
  93.7 0.7 copy.11
  94.3 0.6 copy.12
  95.0 0.6 copy.13
Async XLA Ops:
  0.6 1.6 %copy-start = (f32[2,512,512]{2,1,0:T(8,128)S(1)}, f32[2,512,512]{2,1,0:T(8,128)}, u32[]{:S(2)}) copy-start(f32[2,512,512]{2,1,0:T(8,128)} %dinv_hbm.1) | copy-start | bytes 6291460
  2.2 1.2 %copy-start.1 = (f32[256,1024]{1,0:T(8,128)S(1)}, f32[256,1024]{1,0:T(8,128)}, u32[]{:S(2)}) copy-start(f32[256,1024]{1,0:T(8,128)} %tiles_hbm.1) | copy-start | bytes 3145732
  3.4 1.2 %copy-start.2 = (f32[1,512,512]{2,1,0:T(8,128)S(1)}, f32[1,512,512]{2,1,0:T(8,128)}, u32[]{:S(2)}) copy-start(f32[1,512,512]{2,1,0:T(8,128)} %link_hbm.1) | copy-start | bytes 3145732
  4.7 0.9 copy-start.3
  5.6 0.7 copy-start.4

commit v2 on v1

--- a/solution.py
+++ b/solution.py
@@ -11,6 +11,11 @@
 F32 = jnp.float32
 BF16 = jnp.bfloat16
 CHUNKS = 4
+RING8 = (4, 3, 5, 2, 6, 1, 7)
+PLANE = sorted(
+    ((dx, dy, dc) for dx in range(4) for dy in range(4) for dc in range(2) if dx or dy or dc),
+    key=lambda at: -(min(at[0], 4 - at[0]) + min(at[1], 4 - at[1]) + 0.5 * at[2]),
+)
 
 
 def split(value):
@@ -30,9 +35,9 @@
 
 
 def kernel(
-    tiles_hbm, factor_ref, link_hbm, dinv_hbm, anc_ref,
+    tiles_hbm, factor_hbm, link_hbm, dinv_hbm, anc_hbm,
     off_ref, diag_ref, link_ref,
-    tiles_v, tiles_hi, tiles_lo, first, factor_z, factor_split, part, arrive, rows, pair_factor,
+    anc_ref, tiles_v, tiles_hi, tiles_lo, first, factor_z, factor_split, part, arrive, rows, pair_factor,
     link_v, link_hi, link_lo, dinv0_v, dinv1_v, extra,
     left_buf, right_buf, gram, gram_in, line, line_in, plane, z_in, total, final,
     local_sem, first_sem, spread_sem, pair_sem, one_sem, two_sem, ring_sem, rows_sem,
@@ -76,6 +81,8 @@
     def wait_bytes(ref, sem):
         pltpu.make_async_copy(ref, ref, sem).wait()
 
+    own_pair = local(factor_hbm, pair_factor.at[core], local_sem.at[4])
+    own_anc = local(anc_hbm, anc_ref, local_sem.at[5])
     own_tiles = local(tiles_hbm, tiles_v.at[core], local_sem.at[0])
     own_link = local(link_hbm.at[0], link_v, local_sem.at[1])
     own_dinv0 = local(dinv_hbm.at[0], dinv0_v, local_sem.at[2])
@@ -83,9 +90,13 @@
     own_dinv1 = local(dinv_hbm.at[:, slice_rows], dinv1_v, local_sem.at[3])
 
     barrier = pltpu.get_barrier_semaphore()
-    for step in range(1, 32):
-        pl.semaphore_signal(barrier, inc=1, device_id=(z, lax.rem(p + step, 32)), device_id_type=MESH)
-    for step in range(1, 8):
+    def in_plane(offset):
+        dx, dy, dc = offset
+        return lax.rem(x + dx, 4) * 8 + lax.rem(y + dy, 4) * 2 + (1 - core if dc else core)
+
+    for offset in PLANE:
+        pl.semaphore_signal(barrier, inc=1, device_id=(z, in_plane(offset)), device_id_type=MESH)
+    for step in RING8:
         for other in range(2):
             pl.semaphore_signal(
                 barrier, inc=1, device_id=(lax.rem(z + step, 8), (p // 2) * 2 + other), device_id_type=MESH
@@ -100,25 +111,18 @@
         ty = lax.rem(target // 2, 4)
         lane = tx + number * (ty - tx)
         row = ty + number * (tx - ty)
-        return factor_ref.at[
-            number, pl.ds(pl.multiple_of(row * 8, 8), 8), pl.ds(pl.multiple_of(lane * 128, 128), 128)
+        return pair_factor.at[
+            core, number, pl.ds(pl.multiple_of(row * 8, 8), 8), pl.ds(pl.multiple_of(lane * 128, 128), 128)
         ]
 
-    for step in range(1, 32):
-        target = lax.rem(p + step, 32)
+    own_pair.wait()
+    for offset in PLANE:
+        target = in_plane(offset)
         send_group(tile_of(target), first.at[p], first_sem, (z, target), 0)
     local(tile_of(p), first.at[p], first_sem)
 
     send(tiles_hbm, tiles_v.at[core], pair_sem.at[0], partner)
-    send(factor_ref, pair_factor.at[core], pair_sem.at[1], partner)
-    own_pair = local(factor_ref, pair_factor.at[core], local_sem.at[4])
-
-    wait_bytes(first, first_sem)
-    mine = factor_z.at[a, :, z, b]
-    for step in range(1, 8):
-        dest_z = lax.rem(z + step, 8)
-        send_group(first.at[pl.ds(4 * dest_z, 4)], mine, spread_sem, (dest_z, p), 1)
-    local(first.at[pl.ds(4 * z, 4)], mine, spread_sem)
+    send(pair_factor.at[core], pair_factor.at[core], pair_sem.at[1], partner)
 
     def keep_of(number, row_block):
         listed = anc_ref[number, 0] == row_block
@@ -126,6 +130,7 @@
             listed = jnp.logical_or(listed, anc_ref[number, entry] == row_block)
         return jnp.where(listed, jnp.float32(1), jnp.float32(0))
 
+    own_anc.wait()
     keep_low = keep_of(core, 2 * z)
     keep_high = keep_of(core, 2 * z + 1)
     keep0 = keep_of(0, block)
@@ -157,29 +162,6 @@
         return carry
 
     lax.fori_loop(0, 16, split_link, 0)
-
-    sent[0].wait_recv()
-    split_tiles(1 - core)
-
-    def piece(lane, row):
-        return factor_z.at[lane, :, :, row]
-
-    def half(lane, row, which):
-        return factor_z.at[lane, pl.ds(2 * which, 2), :, row]
-
-    a_next, a_prev, a_far = lax.rem(a + 1, 4), lax.rem(a + 3, 4), lax.rem(a + 2, 4)
-    b_next, b_prev, b_far = lax.rem(b + 1, 4), lax.rem(b + 3, 4), lax.rem(b + 2, 4)
-    to_b_next, to_b_prev = device(z, a, b_next), device(z, a, b_prev)
-    to_a_next, to_a_prev = device(z, a_next, b), device(z, a_prev, b)
-
-    def along_a(row, order):
-        send(piece(a, row), piece(a, row), two_sem.at[0, order], to_a_next)
-        send(piece(a, row), piece(a, row), two_sem.at[1, order], to_a_prev)
-
-    wait_bytes(piece(a, b), spread_sem)
-    send(piece(a, b), piece(a, b), one_sem.at[0], to_b_next)
-    send(piece(a, b), piece(a, b), one_sem.at[1], to_b_prev)
-    along_a(b, 0)
 
     row_ids = lax.broadcasted_iota(jnp.int32, (16, 512), 0) + p * 16
     col_ids = lax.broadcasted_iota(jnp.int32, (16, 512), 1)
@@ -191,14 +173,73 @@
     picked = dot3(split(picked), split(dinv0_v[...]))
     extra[...] = dot3(split(picked), (link_hi[...], link_lo[...]))
 
+    wait_bytes(first, first_sem)
+    mine = factor_z.at[a, b, :, z]
+    for step in RING8:
+        dest_z = lax.rem(z + step, 8)
+        send_group(first.at[pl.ds(4 * dest_z, 4)], mine, spread_sem, (dest_z, p), 1)
+    local(first.at[pl.ds(4 * z, 4)], mine, spread_sem)
+
+    sent[0].wait_recv()
+    split_tiles(1 - core)
+
+    wait_bytes(pair_factor.at[1 - core], pair_sem.at[1])
+
+    def own_rows(number, keep):
+        return jnp.concatenate([pair_factor[0, number], pair_factor[1, number]], axis=0) * keep
+
+    masked0 = own_rows(0, keep0)
+    masked1 = own_rows(1, keep1)
+    link_pair = (link_hi[...], link_lo[...])
+    linked0 = dot3(split(masked0), link_pair)
+
+    def put_left(at, value):
+        high, low = split(value)
+        left_buf[at:at + 64, :] = high
+        left_buf[at + 64:at + 128, :] = high
+        left_buf[at + 128:at + 192, :] = low
+
+    half_cols = pl.ds(pl.multiple_of(core * 256, 256), 256)
+
+    def put_right(at, value):
+        high, low = split(value)
+        right_buf[at:at + 64, :] = high
+        right_buf[at + 64:at + 128, :] = low
+        right_buf[at + 128:at + 192, :] = high
+
+    put_left(0, -masked0)
+    put_left(384, masked1)
+    put_left(768, -linked0)
+
+
+    def piece(lane, row):
+        return factor_z.at[lane, row]
+
+    def half(lane, row, which):
+        return factor_z.at[lane, row, pl.ds(2 * which, 2)]
+
+    a_next, a_prev, a_far = lax.rem(a + 1, 4), lax.rem(a + 3, 4), lax.rem(a + 2, 4)
+    b_next, b_prev, b_far = lax.rem(b + 1, 4), lax.rem(b + 3, 4), lax.rem(b + 2, 4)
+    to_b_next, to_b_prev = device(z, a, b_next), device(z, a, b_prev)
+    to_a_next, to_a_prev = device(z, a_next, b), device(z, a_prev, b)
+
+    def along_a(row, order):
+        send(piece(a, row), piece(a, row), two_sem.at[0, order], to_a_next)
+        send(piece(a, row), piece(a, row), two_sem.at[1, order], to_a_prev)
+
+    wait_bytes(piece(a, b), spread_sem)
+    send(piece(a, b), piece(a, b), one_sem.at[0], to_b_next)
+    send(piece(a, b), piece(a, b), one_sem.at[1], to_b_prev)
+    send(piece(a, b), piece(a, b), one_sem.at[2], device(z, a, b_far))
+    for copy in sent[-3:-1]:
+        copy.wait_send()
+    along_a(b, 0)
+
     wait_bytes(piece(a, b_prev), one_sem.at[0])
-    send(half(a, b_prev, 0), half(a, b_prev, 0), one_sem.at[2], to_b_next)
     along_a(b_prev, 1)
     wait_bytes(piece(a, b_next), one_sem.at[1])
-    send(half(a, b_next, 1), half(a, b_next, 1), one_sem.at[3], to_b_prev)
     along_a(b_next, 2)
-    wait_bytes(half(a, b_far, 0), one_sem.at[2])
-    wait_bytes(half(a, b_far, 1), one_sem.at[3])
+    wait_bytes(piece(a, b_far), one_sem.at[2])
     along_a(b_far, 3)
     row_order = (b, b_prev, b_next, b_far)
 
@@ -211,7 +252,7 @@
 
     def compute(number, lane):
         def prepare(step, carry):
-            value = factor_z[lane, step].reshape(256, 128)
+            value = jnp.stack([factor_z[lane, row, step] for row in range(4)], axis=1).reshape(256, 128)
             value = value * jnp.where(step < 2, keep_low, keep_high)
             high, low = split(value)
             at = pl.ds(pl.multiple_of(step * 256, 256), 256)
@@ -225,7 +266,7 @@
             at = pl.ds(pl.multiple_of(step * 128, 128), 128)
             both = dot(tiles_hi[at, :], factor_split[...])
             result = both[:, 0:128] + both[:, 128:256] + dot(tiles_lo[at, :], factor_split[:, 0:128])
-            part[number, step // 2, pl.ds(lax.rem(step, 2) * 4, 4)] = result.reshape(4, 32, 128)
+            part[number, pl.ds(lax.rem(step, 2) * 4, 4), step // 2] = result.reshape(4, 32, 128)
             return carry
 
         lax.fori_loop(0, 4, multiply, 0)
@@ -241,85 +282,76 @@
             dest = lax.rem(z + forward - step, 8)
             if step:
                 wait_bytes(arrive.at[number, step - 1], ring_sem.at[number, step - 1])
-                part[number, :, dest] = part[number, :, dest] + arrive[number, step - 1]
-            send(part.at[number, :, dest], arrive.at[number, step], ring_sem.at[number, step], to_z_next)
+                part[number, dest] = part[number, dest] + arrive[number, step - 1]
+            send(part.at[number, dest], arrive.at[number, step], ring_sem.at[number, step], to_z_next)
         if step < backward:
             dest = lax.rem(z + 8 - backward + step, 8)
             slot = forward + step
             if step:
                 wait_bytes(arrive.at[number, slot - 1], ring_sem.at[number, slot - 1])
-                part[number, :, dest] = part[number, :, dest] + arrive[number, slot - 1]
-            send(part.at[number, :, dest], arrive.at[number, slot], ring_sem.at[number, slot], to_z_prev)
+                part[number, dest] = part[number, dest] + arrive[number, slot - 1]
+            send(part.at[number, dest], arrive.at[number, slot], ring_sem.at[number, slot], to_z_prev)
+
+    def publish(number, lane, value):
+        rows[core, lane] = value.reshape(64, 128)
+        send(rows.at[core, lane], rows.at[core, lane], rows_sem.at[number], partner)
 
     def ring_end(number, lane):
         forward, _ = hops(number)
         wait_bytes(arrive.at[number, forward - 1], ring_sem.at[number, forward - 1])
         wait_bytes(arrive.at[number, 6], ring_sem.at[number, 6])
-        value = part[number, :, z] + arrive[number, forward - 1] + arrive[number, 6]
-        rows[core, lane] = value.reshape(64, 128)
-        send(rows.at[core, lane], rows.at[core, lane], rows_sem.at[number], partner)
+        publish(number, lane, part[number, z] + arrive[number, forward - 1] + arrive[number, 6])
+
+    def along(distance):
+        return lax.rem(z + 8 + (1 - 2 * core) * distance, 8)
+
+    def pair_send(number, slot, dest, to):
+        send(
+            part.at[number, along(dest)], arrive.at[number, slot], ring_sem.at[number, slot], (along(to), p)
+        )
+
+    def pairs_start(number):
+        pair_send(number, 0, 4, 1)
+        pair_send(number, 1, 2, 1)
+        pair_send(number, 2, -3, -1)
+        pair_send(number, 3, -1, -1)
+
+    def pairs_middle(number):
+        for slot, dest in ((0, 3), (2, -2), (1, 1)):
+            wait_bytes(arrive.at[number, slot], ring_sem.at[number, slot])
+            part[number, along(dest)] = part[number, along(dest)] + arrive[number, slot]
+            pair_send(number, slot + 4, dest, dest)
+
+    def pairs_end(number, lane):
+        value = part[number, z]
+        for slot in range(3, 7):
+            wait_bytes(arrive.at[number, slot], ring_sem.at[number, slot])
+            value = value + arrive[number, slot]
+        publish(number, lane, value)
 
     compute(0, a)
-    ring(0, 0)
+    pairs_start(0)
     relay(0)
     relay(1)
-    ring(0, 1)
     relay(2)
+    pairs_middle(0)
     relay(3)
-    ring(0, 2)
     compute(1, a_prev)
-    ring(1, 0)
-    ring(0, 3)
+    pairs_start(1)
     compute(2, a_next)
-    ring(2, 0)
-    ring(1, 1)
+    pairs_start(2)
+    pairs_end(0, a)
     for order in range(4):
         wait_bytes(half(a_far, row_order[order], 0), two_sem.at[2, order])
         wait_bytes(half(a_far, row_order[order], 1), two_sem.at[3, order])
     compute(3, a_far)
-    ring(3, 0)
-    ring(2, 1)
-    ring(1, 2)
-    ring_end(0, a)
-    ring(3, 1)
-    ring(2, 2)
-    ring(1, 3)
-    ring(3, 2)
-    ring(2, 3)
-    ring_end(1, a_prev)
-    ring(3, 3)
-    ring_end(2, a_next)
-
-    own_pair.wait()
-    wait_bytes(pair_factor.at[1 - core], pair_sem.at[1])
-
-    def own_rows(number, keep):
-        return jnp.concatenate([pair_factor[0, number], pair_factor[1, number]], axis=0) * keep
-
-    masked0 = own_rows(0, keep0)
-    masked1 = own_rows(1, keep1)
-    link_pair = (link_hi[...], link_lo[...])
-    linked0 = dot3(split(masked0), link_pair)
-
-    def put_left(at, value):
-        high, low = split(value)
-        left_buf[at:at + 64, :] = high
-        left_buf[at + 64:at + 128, :] = high
-        left_buf[at + 128:at + 192, :] = low
-
-    half_cols = pl.ds(pl.multiple_of(core * 256, 256), 256)
-
-    def put_right(at, value):
-        high, low = split(value)
-        right_buf[at:at + 64, :] = high
-        right_buf[at + 64:at + 128, :] = low
-        right_buf[at + 128:at + 192, :] = high
-
-    put_left(0, -masked0)
-    put_left(384, masked1)
-    put_left(768, -linked0)
-
-    ring_end(3, a_far)
+    pairs_start(3)
+    pairs_middle(1)
+    pairs_middle(2)
+    pairs_middle(3)
+    pairs_end(1, a_prev)
+    pairs_end(2, a_next)
+    pairs_end(3, a_far)
     for number in range(CHUNKS):
         wait_bytes(rows.at[1 - core, 0], rows_sem.at[number])
 
@@ -426,7 +458,7 @@
     for mat in range(3):
         line_end(mat)
 
-    for step in range(1, 8):
+    for step in RING8:
         dest_z = lax.rem(z + step, 8)
         send_group(plane.at[dest_z], z_in.at[z], z_sem, (dest_z, p), 2)
     local(plane.at[z], z_in.at[z], z_sem)
@@ -438,7 +470,7 @@
     final[8] = value
     owner = z // 4
     slot = lax.rem(z, 4) * 2 + core
-    for step in range(1, 8):
+    for step in RING8:
         send_group(plane_total, final.at[slot], final_sem, (lax.rem(z + step, 8), (p // 2) * 2 + owner), 3)
 
     @pl.when(owner == core)
@@ -463,8 +495,9 @@
     link_ref[0] = -(slice_of(1) + dot3(split(diag0), (link_hi[...], link_lo[...])))
     diag_ref[1] = dinv1_v[1] + extra[...] + slice_of(2)
 
-    for copy in sent:
-        copy.wait_send()
+    for number, copy in enumerate(sent):
+        if number not in (2, 3):
+            copy.wait_send()
     wait_bytes(first.at[pl.ds(0, 31)], group_send.at[0])
     wait_bytes(first.at[pl.ds(0, 28)], group_send.at[1])
     wait_bytes(plane.at[pl.ds(0, 7)], group_send.at[2])
@@ -476,7 +509,7 @@
 
 
 def body(inverse_tiles, factor, link_factor, diag_inverse, ancestors):
-    anywhere = pl.BlockSpec(memory_space=pl.ANY)
+    anywhere = pl.BlockSpec(memory_space=pltpu.MemorySpace.HBM)
     vmem = pl.BlockSpec(memory_space=pltpu.VMEM)
     dma = pltpu.SemaphoreType.DMA
     return pl.pallas_call(
@@ -486,16 +519,17 @@
             jax.ShapeDtypeStruct((2, 16, 512), F32),
             jax.ShapeDtypeStruct((1, 16, 512), F32),
         ),
-        in_specs=[anywhere, vmem, anywhere, anywhere, pl.BlockSpec(memory_space=pltpu.SMEM)],
+        in_specs=[anywhere] * 5,
         out_specs=(vmem, vmem, vmem),
         scratch_shapes=[
+            pltpu.SMEM((2, 8), jnp.int32),
             pltpu.VMEM((2, 256, 1024), F32),
             pltpu.VMEM((512, 1024), BF16),
             pltpu.VMEM((512, 1024), BF16),
             pltpu.VMEM((32, 8, 128), F32),
-            pltpu.VMEM((4, 4, 8, 4, 8, 128), F32),
+            pltpu.VMEM((4, 4, 4, 8, 8, 128), F32),
             pltpu.VMEM((1024, 256), BF16),
-            pltpu.VMEM((CHUNKS, 2, 8, 32, 128), F32),
+            pltpu.VMEM((CHUNKS, 8, 2, 32, 128), F32),
             pltpu.VMEM((CHUNKS, 7, 2, 32, 128), F32),
             pltpu.VMEM((2, 4, 64, 128), F32),
             pltpu.VMEM((2, 2, 32, 512), F32),
@@ -515,7 +549,7 @@
             pltpu.VMEM((8, 3, 8, 128), F32),
             pltpu.VMEM((4, 64, 512), F32),
             pltpu.VMEM((9, 3, 8, 128), F32),
-            dma((5,)),
+            dma((6,)),
             dma,
             dma,
             dma((2,)),
@@ -531,7 +565,7 @@
             dma((5,)),
         ],
         compiler_params=pltpu.CompilerParams(
-            collective_id=0, has_side_effects=True, vmem_limit_bytes=48 * 1024 * 1024
+            collective_id=0, has_side_effects=True, vmem_limit_bytes=67043328
         ),
     )(inverse_tiles, factor, link_factor, diag_inverse, ancestors)
 

time: 95.8 us -> 82.1 us (0.86)
  Pallas kernels: 87.4 us -> 76.8 us
  local copies, waits for them, and re-layouts: 7.52 us -> 4.41 us
    pallas_call x1, Pallas kernels: 87.4 us -> 76.8 us  [body(): pl.pallas_call(kernel, out_shape=(jax.ShapeDtypeStruct((2, 32, 512), F32)...]
    unnamed x13 -> x3, local copies, waits for them, and re-layouts: 7.52 us -> 4.41 us
where the time goes in v2:
time: 82.1 us; the launch traced here: 81.9 us
  Pallas kernels  76.8 us (94%)
  local copies, waits for them, and re-layouts  4.41 us (5%)
    pallas_call x1, Pallas kernels, body(): pl.pallas_call(kernel, out_shape=(jax.ShapeDtypeStruct((2, 32, 512), F32)...  76.8 us
    unnamed x3, local copies, waits for them, and re-layouts  4.41 us

profile of v2, /device:TPU:1, one launch (start us, length us, event | category | flops | bytes accessed | tf_op | source)
XLA Modules:
  0.0 81.9 jit_solution(6243468836225173926)
XLA Ops:
  0.6 76.8 %shard_map.76 = (f32[2,32,512]{2,1,0:T(8,128)}, f32[2,16,512]{2,1,0:T(8,128)}, f32[1,16,512]{2,1,0:T(8,128)}) custom-call(f32[256,1024]{1,0:T(8,128)} %tiles_hbm.1, f32[2,32,512]{2,1,0:T(8,128)} %factor_hbm.1, f32[1,512,512]{2,1,0:T(8,128)} %link_hbm.1, f32[2,512,512]{2,1,0:T(8,128)} %dinv_hbm.1, s32[2,8]{1,0:T(2,128)} %anc_hbm.1), custom_call_target="tpu_custom_call" | custom-call | tf_op jit(solution)/shard_map/pallas_call | solution.py:515
  77.5 1.6 %copy.11 = f32[2,32,512]{2,1,0:T(8,128)} copy(f32[2,32,512]{2,1,0:T(8,128)} %get-tuple-element.6) | data formatting | bytes 262144
  79.0 1.5 %copy.12 = f32[2,16,512]{2,1,0:T(8,128)} copy(f32[2,16,512]{2,1,0:T(8,128)} %get-tuple-element.7) | data formatting | bytes 131072
  80.5 1.4 %copy.13 = f32[1,16,512]{2,1,0:T(8,128)} copy(f32[1,16,512]{2,1,0:T(8,128)} %get-tuple-element.8) | data formatting | bytes 65536

commit v3 on v2

v3 whole, which is shorter than its diff:
```python
import functools

import jax
import jax.numpy as jnp
from jax import lax
from jax.experimental import pallas as pl
from jax.experimental.pallas import tpu as pltpu
from jax.sharding import PartitionSpec as P

MESH = pl.DeviceIdType.MESH
F32 = jnp.float32
BF16 = jnp.bfloat16
CHUNKS = 4
RING8 = (4, 3, 5, 2, 6, 1, 7)
PLANE = sorted(
    ((dx, dy, dc) for dx in range(4) for dy in range(4) for dc in range(2) if dx or dy or dc),
    key=lambda at: -(min(at[0], 4 - at[0]) + min(at[1], 4 - at[1]) + 0.5 * at[2]),
)


def split(value):
    high = value.astype(BF16)
    low = (value - high.astype(F32)).astype(BF16)
    return high, low


def dot(left, right):
    return jnp.dot(left, right, preferred_element_type=F32)


def dot3(left, right):
    left_high, left_low = left
    right_high, right_low = right
    return dot(left_high, right_high) + dot(left_high, right_low) + dot(left_low, right_high)


def kernel(
    tiles_hbm, factor_hbm, link_hbm, dinv_hbm, anc_hbm,
    out_ref,
    anc_ref, tiles_v, tiles_hi, tiles_lo, first, factor_z, factor_split, part, arrive, rows, pair_factor,
    link_v, link_hi, link_lo, dinv0_v, dinv1_v, extra,
    left_buf, right_buf, gram, gram_in, line, line_in, plane, z_in, total, final,
    local_sem, first_sem, spread_sem, pair_sem, one_sem, two_sem, far_sem, ring_sem, rows_sem,
    gram_sem, line_sem, z_sem, final_sem, group_send,
):
    z = lax.axis_index("prow")
    p = lax.axis_index("pcol")
    core = lax.rem(p, 2)
    x = p // 8
    y = lax.rem(p // 2, 4)
    a = x + core * (y - x)
    b = y + core * (x - y)
    block = p // 2

    def device(dest_z, dest_a, dest_b):
        dest_x = dest_a + core * (dest_b - dest_a)
        dest_y = dest_b + core * (dest_a - dest_b)
        return (dest_z, (dest_x * 4 + dest_y) * 2 + core)

    def local(src, dst, sem):
        copy = pltpu.make_async_copy(src, dst, sem)
        copy.start()
        return copy

    def send(src, dst, recv, target, group):
        pltpu.make_async_remote_copy(
            src_ref=src, dst_ref=dst, send_sem=group_send.at[group], recv_sem=recv,
            device_id=target, device_id_type=MESH,
        ).start()

    def wait_bytes(ref, sem):
        pltpu.make_async_copy(ref, ref, sem).wait()

    own_pair = local(factor_hbm, pair_factor.at[core], local_sem.at[4])
    own_anc = local(anc_hbm, anc_ref, local_sem.at[5])
    own_tiles = local(tiles_hbm, tiles_v.at[core], local_sem.at[0])
    own_link = local(link_hbm.at[0], link_v, local_sem.at[1])
    own_dinv0 = local(dinv_hbm.at[0], dinv0_v, local_sem.at[2])
    slice_rows = pl.ds(pl.multiple_of(p * 16, 16), 16)
    own_dinv1 = local(dinv_hbm.at[:, slice_rows], dinv1_v, local_sem.at[3])

    barrier = pltpu.get_barrier_semaphore()
    def in_plane(offset):
        dx, dy, dc = offset
        return lax.rem(x + dx, 4) * 8 + lax.rem(y + dy, 4) * 2 + (1 - core if dc else core)

    for offset in PLANE:
        pl.semaphore_signal(barrier, inc=1, device_id=(z, in_plane(offset)), device_id_type=MESH)
    for step in RING8:
        for other in range(2):
            pl.semaphore_signal(
                barrier, inc=1, device_id=(lax.rem(z + step, 8), (p // 2) * 2 + other), device_id_type=MESH
            )
    pl.semaphore_wait(barrier, 31 + 14)

    partner = (z, p + 1 - 2 * core)

    def tile_of(target):
        number = lax.rem(target, 2)
        tx = target // 8
        ty = lax.rem(target // 2, 4)
        lane = tx + number * (ty - tx)
        row = ty + number * (tx - ty)
        return pair_factor.at[
            core, number, pl.ds(pl.multiple_of(row * 8, 8), 8), pl.ds(pl.multiple_of(lane * 128, 128), 128)
        ]

    own_pair.wait()
    for offset in PLANE:
        target = in_plane(offset)
        send(tile_of(target), first.at[p], first_sem, (z, target), 0)
    local(tile_of(p), first.at[p], first_sem)

    send(tiles_hbm, tiles_v.at[core], pair_sem.at[0], partner, 5)
    send(pair_factor.at[core], pair_factor.at[core], pair_sem.at[1], partner, 6)

    def keep_of(number, row_block):
        listed = anc_ref[number, 0] == row_block
        for entry in range(1, anc_ref.shape[1]):
            listed = jnp.logical_or(listed, anc_ref[number, entry] == row_block)
        return jnp.where(listed, jnp.float32(1), jnp.float32(0))

    own_anc.wait()
    keep_low = keep_of(core, 2 * z)
    keep_high = keep_of(core, 2 * z + 1)
    keep0 = keep_of(0, block)
    keep1 = keep_of(1, block)

    own_tiles.wait()

    def split_tiles(half):
        def go(step, carry):
            at = pl.ds(pl.multiple_of(step * 32, 32), 32)
            high, low = split(tiles_v[half, at, :])
            put = pl.ds(pl.multiple_of(half * 256 + step * 32, 32), 32)
            tiles_hi[put, :] = high
            tiles_lo[put, :] = low
            return carry

        lax.fori_loop(0, 8, go, 0)

    split_tiles(core)
    own_link.wait()
    own_dinv0.wait()
    own_dinv1.wait()

    def split_link(step, carry):
        at = pl.ds(pl.multiple_of(step * 32, 32), 32)
        high, low = split(link_v[at, :])
        link_hi[at, :] = high
        link_lo[at, :] = low
        return carry

    lax.fori_loop(0, 16, split_link, 0)

    row_ids = lax.broadcasted_iota(jnp.int32, (16, 512), 0) + p * 16
    col_ids = lax.broadcasted_iota(jnp.int32, (16, 512), 1)
    pick = jnp.where(row_ids == col_ids, jnp.float32(1), jnp.float32(0)).astype(BF16)
    across = (((1,), (1,)), ((), ()))
    picked = lax.dot_general(pick, link_hi[...], across, preferred_element_type=F32) + lax.dot_general(
        pick, link_lo[...], across, preferred_element_type=F32
    )
    picked = dot3(split(picked), split(dinv0_v[...]))
    extra[0] = dot3(split(picked), (link_hi[...], link_lo[...]))
    extra[1] = dot3(split(dinv1_v[0]), (link_hi[...], link_lo[...]))

    wait_bytes(first, first_sem)
    mine = factor_z.at[a, b, :, z]
    for step in RING8:
        dest_z = lax.rem(z + step, 8)
        send(first.at[pl.ds(4 * dest_z, 4)], mine, spread_sem, (dest_z, p), 1)
    local(first.at[pl.ds(4 * z, 4)], mine, spread_sem)

    wait_bytes(tiles_v.at[1 - core], pair_sem.at[0])
    split_tiles(1 - core)

    wait_bytes(pair_factor.at[1 - core], pair_sem.at[1])

    def own_rows(number, keep):
        return jnp.concatenate([pair_factor[0, number], pair_factor[1, number]], axis=0) * keep

    masked0 = own_rows(0, keep0)
    masked1 = own_rows(1, keep1)
    link_pair = (link_hi[...], link_lo[...])
    linked0 = dot3(split(masked0), link_pair)

    def put(buffer, segment, terms):
        for number, term in enumerate(terms):
            at = segment * 192 + number * 64
            buffer[at:at + 64, :] = term

    def put_left(segment, value):
        high, low = split(value)
        put(left_buf, segment, (high, high, low))

    half_cols = pl.ds(pl.multiple_of(core * 256, 256), 256)

    def put_right(segments, number):
        high, low = split(total[number, :, half_cols])
        for segment in segments:
            put(right_buf, segment, (high, low, high))

    total[3] = masked1
    put_left(0, -masked0)
    put_left(2, masked1)
    put_left(4, -linked0)
    put_right((2, 4), 3)

    def piece(lane, row):
        return factor_z.at[lane, row]

    def half(lane, row, which):
        return factor_z.at[lane, row, pl.ds(2 * which, 2)]

    a_next, a_prev, a_far = lax.rem(a + 1, 4), lax.rem(a + 3, 4), lax.rem(a + 2, 4)
    b_next, b_prev, b_far = lax.rem(b + 1, 4), lax.rem(b + 3, 4), lax.rem(b + 2, 4)
    to_b_next, to_b_prev = device(z, a, b_next), device(z, a, b_prev)
    to_a_next, to_a_prev = device(z, a_next, b), device(z, a_prev, b)

    def along_a(row, order):
        send(piece(a, row), piece(a, row), two_sem.at[0, order], to_a_next, 8)
        send(piece(a, row), piece(a, row), two_sem.at[1, order], to_a_prev, 8)

    wait_bytes(piece(a, b), spread_sem)
    send(piece(a, b), piece(a, b), one_sem.at[0], to_b_next, 7)
    send(piece(a, b), piece(a, b), one_sem.at[1], to_b_prev, 7)
    send(piece(a, b), piece(a, b), one_sem.at[2], device(z, a, b_far), 13)
    along_a(b, 0)
    row_order = (b, b_prev, b_next, b_far)

    def relay(order):
        row = row_order[order]
        wait_bytes(piece(a_prev, row), two_sem.at[0, order])
        send(half(a_prev, row, 0), half(a_prev, row, 0), far_sem, to_a_next, 8)
        wait_bytes(piece(a_next, row), two_sem.at[1, order])
        send(half(a_next, row, 1), half(a_next, row, 1), far_sem, to_a_prev, 8)

    wait_bytes(piece(a, b_prev), one_sem.at[0])
    along_a(b_prev, 1)
    wait_bytes(piece(a, b_next), one_sem.at[1])
    along_a(b_next, 2)
    relay(0)
    wait_bytes(piece(a, b_far), one_sem.at[2])
    along_a(b_far, 3)
    send(piece(a, b_far), piece(a, b_far), far_sem, device(z, a_far, b), 8)
    relay(1)

    def compute(number, lane):
        def prepare(step, carry):
            value = jnp.stack([factor_z[lane, row, step] for row in range(4)], axis=1).reshape(256, 128)
            value = value * jnp.where(step < 2, keep_low, keep_high)
            high, low = split(value)
            at = pl.ds(pl.multiple_of(step * 256, 256), 256)
            factor_split[at, 0:128] = high
            factor_split[at, 128:256] = low
            return carry

        lax.fori_loop(0, 4, prepare, 0)

        def multiply(step, carry):
            at = pl.ds(pl.multiple_of(step * 256, 256), 256)
            both = dot(tiles_hi[at, :], factor_split[...])
            result = both[:, 0:128] + both[:, 128:256] + dot(tiles_lo[at, :], factor_split[:, 0:128])
            part[number, :, step] = result.reshape(8, 32, 128)
            return carry

        lax.fori_loop(0, 2, multiply, 0)

    def publish(number, lane, value):
        rows[core, lane] = value.reshape(64, 128)
        send(rows.at[core, lane], rows.at[core, lane], rows_sem, partner, 10)

    def along(distance):
        return lax.rem(z + 8 + (1 - 2 * core) * distance, 8)

    def pair_send(number, slot, dest, to):
        send(
            part.at[number, along(dest)], arrive.at[number, slot], ring_sem.at[number, min(slot, 3)], (along(to), p), 9
        )

    def pairs_start(number):
        pair_send(number, 0, 4, 1)
        pair_send(number, 1, 2, 1)
        pair_send(number, 2, -3, -1)
        pair_send(number, 3, -1, -1)

    def pairs_middle(number):
        for slot, dest in ((0, 3), (2, -2), (1, 1)):
            wait_bytes(arrive.at[number, slot], ring_sem.at[number, slot])
            part[number, along(dest)] = part[number, along(dest)] + arrive[number, slot]
            pair_send(number, slot + 4, dest, dest)

    def pairs_end(number, lane):
        wait_bytes(arrive.at[number, pl.ds(3, 4)], ring_sem.at[number, 3])
        value = part[number, z]
        for slot in range(3, 7):
            value = value + arrive[number, slot]
        publish(number, lane, value)

    compute(0, a)
    pairs_start(0)
    relay(2)
    pairs_middle(0)
    wait_bytes(piece(a_prev, b_far), two_sem.at[0, 3])
    wait_bytes(piece(a_next, b_far), two_sem.at[1, 3])
    compute(1, a_prev)
    pairs_start(1)
    compute(2, a_next)
    pairs_start(2)
    pairs_end(0, a)
    wait_bytes(factor_z.at[a_far], far_sem)
    compute(3, a_far)
    pairs_start(3)
    pairs_middle(1)
    pairs_middle(2)
    pairs_middle(3)
    pairs_end(1, a_prev)
    pairs_end(2, a_next)
    pairs_end(3, a_far)
    wait_bytes(rows.at[1 - core], rows_sem)

    def joined(number):
        return jnp.concatenate([rows[number, lane] for lane in range(4)], axis=1)

    flip = (((0,), (0,)), ((), ()))

    def product(mat, left_segment, right_segment, segments, swap):
        def go(step, carry):
            lanes = pl.ds(pl.multiple_of(step * 128, 128), 128)
            value = lax.dot_general(
                left_buf[left_segment * 192:(left_segment + segments) * 192, lanes],
                right_buf[right_segment * 192:(right_segment + segments) * 192, :],
                flip, preferred_element_type=F32,
            )
            for inner in range(4):
                upper = step + swap * (inner - step)
                lower = inner + swap * (step - inner)
                gram[mat, upper, lower] = value[inner * 32:(inner + 1) * 32, :]
            return carry

        lax.fori_loop(0, 4, go, 0)

    own_first = (a, b, a)
    own_second = (b, a, b)
    next_first = (to_a_next, to_b_next, to_a_next)
    prev_first = (to_a_prev, to_b_prev, to_a_prev)

    def gram_start(mat):
        up = lax.rem(own_first[mat] + 1, 4)
        down = lax.rem(own_first[mat] + 3, 4)
        far = lax.rem(own_first[mat] + 2, 4)
        low, high = pl.ds(0, 2), pl.ds(2, 2)
        send(gram.at[mat, far, low], gram_in.at[mat, 0], gram_sem.at[mat, 0], next_first[mat], 11)
        send(gram.at[mat, far, high], gram_in.at[mat, 1], gram_sem.at[mat, 1], prev_first[mat], 11)
        send(gram.at[mat, up, high], gram_in.at[mat, 2], gram_sem.at[mat, 2], next_first[mat], 11)
        send(gram.at[mat, down, low], gram_in.at[mat, 3], gram_sem.at[mat, 2], prev_first[mat], 11)

    def gram_middle(mat):
        up = lax.rem(own_first[mat] + 1, 4)
        down = lax.rem(own_first[mat] + 3, 4)
        low, high = pl.ds(0, 2), pl.ds(2, 2)
        wait_bytes(gram_in.at[mat, 0], gram_sem.at[mat, 0])
        gram[mat, up, low] = gram[mat, up, low] + gram_in[mat, 0]
        send(gram.at[mat, up, low], gram_in.at[mat, 4], gram_sem.at[mat, 2], next_first[mat], 11)
        wait_bytes(gram_in.at[mat, 1], gram_sem.at[mat, 1])
        gram[mat, down, high] = gram[mat, down, high] + gram_in[mat, 1]
        send(gram.at[mat, down, high], gram_in.at[mat, 5], gram_sem.at[mat, 2], prev_first[mat], 11)

    def gram_end(mat):
        here = own_first[mat]
        low, high = pl.ds(0, 2), pl.ds(2, 2)
        wait_bytes(gram_in.at[mat, pl.ds(2, 4)], gram_sem.at[mat, 2])
        line[mat, low] = gram[mat, here, low] + gram_in[mat, 3] + gram_in[mat, 4]
        line[mat, high] = gram[mat, here, high] + gram_in[mat, 2] + gram_in[mat, 5]
        for step in range(1, 4):
            other = lax.rem(own_second[mat] + step, 4)
            target = device(z, a, other) if mat != 1 else device(z, other, b)
            send(line.at[mat, other], line_in.at[mat, step - 1], line_sem.at[mat], target, 12)

    def line_end(mat):
        wait_bytes(line_in.at[mat], line_sem.at[mat])
        value = line[mat, own_second[mat]] + line_in[mat, 0] + line_in[mat, 1] + line_in[mat, 2]
        for row in range(4):
            for lane in range(2):
                plane[2 * row + lane, mat] = value[row * 8:(row + 1) * 8, lane * 128:(lane + 1) * 128]

    off0 = joined(0) * (-keep0)
    total[0] = off0
    put_right((0,), 0)
    product(0, 0, 0, 1, core)
    gram_start(0)

    put_left(1, off0)
    shifted = dot3(split(off0), link_pair)
    total[1] = shifted
    put_right((1, 5), 1)
    product(1, 0, 1, 2, 1 - core)
    gram_start(1)

    put_left(3, shifted)
    total[2] = joined(1) + shifted
    put_right((3,), 2)
    product(2, 2, 3, 3, core)
    gram_start(2)

    mine_rows = pl.ds(pl.multiple_of(core * 32, 32), 32)
    out_ref[0:32] = total[0, mine_rows, :]
    out_ref[32:64] = total[2, mine_rows, :] * (-keep1)

    for mat in range(3):
        gram_middle(mat)
    for mat in range(3):
        gram_end(mat)
    for mat in range(3):
        line_end(mat)

    for step in RING8:
        dest_z = lax.rem(z + step, 8)
        send(plane.at[dest_z], z_in.at[z], z_sem, (dest_z, p), 2)
    local(plane.at[z], z_in.at[z], z_sem)
    wait_bytes(z_in, z_sem)
    value = z_in[0]
    for other in range(1, 8):
        value = value + z_in[other]
    plane_total = final.at[8]
    final[8] = value
    owner = z // 4
    slot = lax.rem(z, 4) * 2 + core
    for step in RING8:
        send(plane_total, final.at[slot], final_sem, (lax.rem(z + step, 8), (p // 2) * 2 + owner), 3)

    @pl.when(owner == core)
    def _():
        local(plane_total, final.at[slot], final_sem)

    @pl.when(owner != core)
    def _():
        send(plane_total, final.at[slot], final_sem, partner, 4)

    wait_bytes(final.at[pl.ds(0, 8)], final_sem)

    def slice_of(mat):
        tiles = []
        for row in range(2):
            lanes = [final[(2 * row + lane) * 2 + side, mat] for side in range(2) for lane in range(2)]
            tiles.append(jnp.concatenate(lanes, axis=1))
        return jnp.concatenate(tiles, axis=0)

    out_ref[64:80] = dinv1_v[0] + slice_of(0)
    out_ref[80:96] = dinv1_v[1] + extra[0] + slice_of(2)
    out_ref[96:112] = -(extra[1] + slice_of(1))

    wait_bytes(factor_z.at[0, pl.ds(0, 2)], group_send.at[7])
    wait_bytes(tiles_v.at[0], group_send.at[5])
    wait_bytes(pair_factor.at[0], group_send.at[6])
    wait_bytes(factor_z.at[pl.ds(0, 3)], group_send.at[8])
    wait_bytes(arrive, group_send.at[9])
    wait_bytes(rows.at[0], group_send.at[10])
    wait_bytes(gram_in, group_send.at[11])
    wait_bytes(line_in, group_send.at[12])
    wait_bytes(factor_z.at[0, 0], group_send.at[13])
    wait_bytes(first.at[pl.ds(0, 31)], group_send.at[0])
    wait_bytes(first.at[pl.ds(0, 28)], group_send.at[1])
    wait_bytes(plane.at[pl.ds(0, 7)], group_send.at[2])
    wait_bytes(plane.at[pl.ds(0, 7)], group_send.at[3])

    @pl.when(owner != core)
    def _():
        wait_bytes(plane.at[0], group_send.at[4])


def part_out(all_ref, off_ref, diag_ref, link_ref):
    off_ref[...] = all_ref[0:64].reshape(2, 32, 512)
    diag_ref[...] = all_ref[64:96].reshape(2, 16, 512)
    link_ref[...] = all_ref[96:112].reshape(1, 16, 512)


def body(inverse_tiles, factor, link_factor, diag_inverse, ancestors):
    anywhere = pl.BlockSpec(memory_space=pltpu.MemorySpace.HBM)
    vmem = pl.BlockSpec(memory_space=pltpu.VMEM)
    dma = pltpu.SemaphoreType.DMA
    out = pl.pallas_call(
        kernel,
        out_shape=jax.ShapeDtypeStruct((112, 512), F32),
        in_specs=[anywhere] * 5,
        out_specs=vmem,
        scratch_shapes=[
            pltpu.SMEM((2, 8), jnp.int32),
            pltpu.VMEM((2, 256, 1024), F32),
            pltpu.VMEM((512, 1024), BF16),
            pltpu.VMEM((512, 1024), BF16),
            pltpu.VMEM((32, 8, 128), F32),
            pltpu.VMEM((4, 4, 4, 8, 8, 128), F32),
            pltpu.VMEM((1024, 256), BF16),
            pltpu.VMEM((CHUNKS, 8, 2, 32, 128), F32),
            pltpu.VMEM((CHUNKS, 7, 2, 32, 128), F32),
            pltpu.VMEM((2, 4, 64, 128), F32),
            pltpu.VMEM((2, 2, 32, 512), F32),
            pltpu.VMEM((512, 512), F32),
            pltpu.VMEM((512, 512), BF16),
            pltpu.VMEM((512, 512), BF16),
            pltpu.VMEM((512, 512), F32),
            pltpu.VMEM((2, 16, 512), F32),
            pltpu.VMEM((2, 16, 512), F32),
            pltpu.VMEM((960, 512), BF16),
            pltpu.VMEM((1152, 256), BF16),
            pltpu.VMEM((3, 4, 4, 32, 256), F32),
            pltpu.VMEM((3, 6, 2, 32, 256), F32),
            pltpu.VMEM((3, 4, 32, 256), F32),
            pltpu.VMEM((3, 3, 32, 256), F32),
            pltpu.VMEM((8, 3, 8, 128), F32),
            pltpu.VMEM((8, 3, 8, 128), F32),
            pltpu.VMEM((4, 64, 512), F32),
            pltpu.VMEM((9, 3, 8, 128), F32),
            dma((6,)),
            dma,
            dma,
            dma((2,)),
            dma((3,)),
            dma((2, 4)),
            dma,
            dma((CHUNKS, 4)),
            dma,
            dma((3, 3)),
            dma((3,)),
            dma,
            dma,
            dma((14,)),
        ],
        compiler_params=pltpu.CompilerParams(
            collective_id=0, has_side_effects=True, vmem_limit_bytes=67043328
        ),
    )(inverse_tiles, factor, link_factor, diag_inverse, ancestors)
    return pl.pallas_call(
        part_out,
        out_shape=(
            jax.ShapeDtypeStruct((2, 32, 512), F32),
            jax.ShapeDtypeStruct((2, 16, 512), F32),
            jax.ShapeDtypeStruct((1, 16, 512), F32),
        ),
        in_specs=[vmem],
        out_specs=(vmem, vmem, vmem),
    )(out)


def solution(mesh):
    in_specs = (P("pcol", "prow"), P(None, ("pcol", "prow"), None), P(), P(), P())
    out_specs = (P(None, ("pcol", "prow"), None), P(None, "pcol", None), P(None, "pcol", None))
    return jax.shard_map(body, mesh=mesh, in_specs=in_specs, out_specs=out_specs, check_vma=False)
```

time: 82.1 us -> 77.8 us (0.948)
  local copies, waits for them, and re-layouts: 4.41 us -> 0 us
    unnamed x3 -> x0, local copies, waits for them, and re-layouts: 4.41 us -> none
    pallas_call x1 -> x2, Pallas kernels: 76.8 us -> 77 us  [the longest x1 75.4 us: body(): pl.pallas_call(kernel, out_shape=jax.ShapeDtypeStruct((112, 512), F32), i...]
where the time goes in v3:
time: 77.8 us; the launch traced here: 77.6 us
  Pallas kernels  77 us (99%)
    pallas_call x1, Pallas kernels, body(): pl.pallas_call(kernel, out_shape=jax.ShapeDtypeStruct((112, 512), F32), i...  75.4 us
    pallas_call x1, Pallas kernels, body(): pl.pallas_call(part_out, out_shape=(jax.ShapeDtypeStruct((2, 32, 512), F3...  1.62 us

profile of v3, /device:TPU:1, one launch (start us, length us, event | category | flops | bytes accessed | tf_op | source)
XLA Modules:
  0.0 77.6 jit_solution(18258591966083582564)
XLA Ops:
  0.6 75.4 %shard_map.76.all_ref = f32[112,512]{1,0:T(8,128)} custom-call(f32[256,1024]{1,0:T(8,128)} %tiles_hbm.1, f32[2,32,512]{2,1,0:T(8,128)} %factor_hbm.1, f32[1,512,512]{2,1,0:T(8,128)} %link_hbm.1, f32[2,512,512]{2,1,0:T(8,128)} %dinv_hbm.1, s32[2,8]{1,0:T(2,128)} %anc_hbm.1), custom_call_target="tpu_custom_call" | custom-call | tf_op jit(solution)/shard_map/pallas_call | solution.py:482
  76.0 1.6 %shard_map.77 = (f32[2,32,512]{2,1,0:T(8,128)}, f32[2,16,512]{2,1,0:T(8,128)}, f32[1,16,512]{2,1,0:T(8,128)}) custom-call(f32[112,512]{1,0:T(8,128)} %shard_map.76.all_ref), custom_call_target="tpu_custom_call" | custom-call | tf_op jit(solution)/shard_map/pallas_call | solution.py:534

commit v4 on v3

--- a/solution.py
+++ b/solution.py
@@ -87,11 +87,8 @@
     for offset in PLANE:
         pl.semaphore_signal(barrier, inc=1, device_id=(z, in_plane(offset)), device_id_type=MESH)
     for step in RING8:
-        for other in range(2):
-            pl.semaphore_signal(
-                barrier, inc=1, device_id=(lax.rem(z + step, 8), (p // 2) * 2 + other), device_id_type=MESH
-            )
-    pl.semaphore_wait(barrier, 31 + 14)
+        pl.semaphore_signal(barrier, inc=1, device_id=(lax.rem(z + step, 8), p), device_id_type=MESH)
+    pl.semaphore_wait(barrier, 31 + 7)
 
     partner = (z, p + 1 - 2 * core)
 
@@ -326,19 +323,21 @@
 
     def product(mat, left_segment, right_segment, segments, swap):
         def go(step, carry):
-            lanes = pl.ds(pl.multiple_of(step * 128, 128), 128)
+            lanes = pl.ds(pl.multiple_of(step * 256, 256), 256)
             value = lax.dot_general(
                 left_buf[left_segment * 192:(left_segment + segments) * 192, lanes],
                 right_buf[right_segment * 192:(right_segment + segments) * 192, :],
                 flip, preferred_element_type=F32,
             )
-            for inner in range(4):
-                upper = step + swap * (inner - step)
-                lower = inner + swap * (step - inner)
-                gram[mat, upper, lower] = value[inner * 32:(inner + 1) * 32, :]
+            for number in range(8):
+                line_x = 2 * step + number // 4
+                line_y = number % 4
+                upper = line_x + swap * (line_y - line_x)
+                lower = line_y + swap * (line_x - line_y)
+                gram[mat, upper, lower] = value[number * 32:(number + 1) * 32, :]
             return carry
 
-        lax.fori_loop(0, 4, go, 0)
+        lax.fori_loop(0, 2, go, 0)
 
     own_first = (a, b, a)
     own_second = (b, a, b)
@@ -391,7 +390,9 @@
     gram_start(0)
 
     put_left(1, off0)
-    shifted = dot3(split(off0), link_pair)
+    off0_high, off0_low = split(off0)
+    both = dot(jnp.concatenate([off0_high, off0_low], axis=0), link_hi[...])
+    shifted = both[0:64] + both[64:128] + dot(off0_high, link_lo[...])
     total[1] = shifted
     put_right((1, 5), 1)
     product(1, 0, 1, 2, 1 - core)
@@ -469,10 +470,18 @@
         wait_bytes(plane.at[0], group_send.at[4])
 
 
-def part_out(all_ref, off_ref, diag_ref, link_ref):
-    off_ref[...] = all_ref[0:64].reshape(2, 32, 512)
-    diag_ref[...] = all_ref[64:96].reshape(2, 16, 512)
-    link_ref[...] = all_ref[96:112].reshape(1, 16, 512)
+def part_out(all_ref, off_ref, diag_ref, link_ref, sems):
+    copies = []
+    at = 0
+    for ref in (off_ref, diag_ref, link_ref):
+        for number in range(ref.shape[0]):
+            rows = ref.shape[1]
+            copies.append(pltpu.make_async_copy(all_ref.at[at:at + rows], ref.at[number], sems.at[len(copies)]))
+            at += rows
+    for copy in copies:
+        copy.start()
+    for copy in copies:
+        copy.wait()
 
 
 def body(inverse_tiles, factor, link_factor, diag_inverse, ancestors):
@@ -539,7 +548,8 @@
             jax.ShapeDtypeStruct((1, 16, 512), F32),
         ),
         in_specs=[vmem],
-        out_specs=(vmem, vmem, vmem),
+        out_specs=(anywhere, anywhere, anywhere),
+        scratch_shapes=[dma((5,))],
     )(out)
 
 

time: 77.8 us -> 76.6 us (0.985)
  Pallas kernels: 77 us -> 75.9 us
    pallas_call x1, Pallas kernels: 75.4 us -> 74.2 us  [body(): pl.pallas_call(kernel, out_shape=jax.ShapeDtypeStruct((112, 512), F32), i...]
where the time goes in v4:
time: 76.6 us; the launch traced here: 76.5 us
  Pallas kernels  75.9 us (99%)
    pallas_call x1, Pallas kernels, body(): pl.pallas_call(kernel, out_shape=jax.ShapeDtypeStruct((112, 512), F32), i...  74.2 us
    pallas_call x1, Pallas kernels, body(): pl.pallas_call(part_out, out_shape=(jax.ShapeDtypeStruct((2, 32, 512), F3...  1.66 us

profile of v4, /device:TPU:1, one launch (start us, length us, event | category | flops | bytes accessed | tf_op | source)
XLA Modules:
  0.0 76.5 jit_solution(4141619931247909734)
XLA Ops:
  0.6 74.2 %shard_map.76.all_ref = f32[112,512]{1,0:T(8,128)} custom-call(f32[256,1024]{1,0:T(8,128)} %tiles_hbm.1, f32[2,32,512]{2,1,0:T(8,128)} %factor_hbm.1, f32[1,512,512]{2,1,0:T(8,128)} %link_hbm.1, f32[2,512,512]{2,1,0:T(8,128)} %dinv_hbm.1, s32[2,8]{1,0:T(2,128)} %anc_hbm.1), custom_call_target="tpu_custom_call" | custom-call | tf_op jit(solution)/shard_map/pallas_call | solution.py:491
  74.9 1.7 %shard_map.77 = (f32[2,32,512]{2,1,0:T(8,128)}, f32[2,16,512]{2,1,0:T(8,128)}, f32[1,16,512]{2,1,0:T(8,128)}) custom-call(f32[112,512]{1,0:T(8,128)} %shard_map.76.all_ref), custom_call_target="tpu_custom_call" | custom-call | tf_op jit(solution)/shard_map/pallas_call | solution.py:543

commit v5 on v4

--- a/solution.py
+++ b/solution.py
@@ -254,14 +254,10 @@
 
         lax.fori_loop(0, 4, prepare, 0)
 
-        def multiply(step, carry):
-            at = pl.ds(pl.multiple_of(step * 256, 256), 256)
-            both = dot(tiles_hi[at, :], factor_split[...])
-            result = both[:, 0:128] + both[:, 128:256] + dot(tiles_lo[at, :], factor_split[:, 0:128])
-            part[number, :, step] = result.reshape(8, 32, 128)
-            return carry
-
-        lax.fori_loop(0, 2, multiply, 0)
+        both = dot(tiles_hi[...], factor_split[...])
+        result = both[:, 0:128] + both[:, 128:256] + dot(tiles_lo[...], factor_split[:, 0:128])
+        for upper in range(2):
+            part[number, :, upper] = result[upper * 256:(upper + 1) * 256].reshape(8, 32, 128)
 
     def publish(number, lane, value):
         rows[core, lane] = value.reshape(64, 128)

time: 76.6 us -> 76.6 us (level)
  no operation moved by 1% of the time
where the time goes in v5:
time: 76.6 us; the launch traced here: 76.5 us
  Pallas kernels  75.8 us (99%)
    pallas_call x1, Pallas kernels, body(): pl.pallas_call(kernel, out_shape=jax.ShapeDtypeStruct((112, 512), F32), i...  74.2 us
    pallas_call x1, Pallas kernels, body(): pl.pallas_call(part_out, out_shape=(jax.ShapeDtypeStruct((2, 32, 512), F3...  1.66 us

profile of v5, /device:TPU:1, one launch (start us, length us, event | category | flops | bytes accessed | tf_op | source)
XLA Modules:
  0.0 76.5 jit_solution(9083064658104250568)
XLA Ops:
  0.6 74.2 %shard_map.76.all_ref = f32[112,512]{1,0:T(8,128)} custom-call(f32[256,1024]{1,0:T(8,128)} %tiles_hbm.1, f32[2,32,512]{2,1,0:T(8,128)} %factor_hbm.1, f32[1,512,512]{2,1,0:T(8,128)} %link_hbm.1, f32[2,512,512]{2,1,0:T(8,128)} %dinv_hbm.1, s32[2,8]{1,0:T(2,128)} %anc_hbm.1), custom_call_target="tpu_custom_call" | custom-call | tf_op jit(solution)/shard_map/pallas_call | solution.py:487
  74.8 1.7 %shard_map.77 = (f32[2,32,512]{2,1,0:T(8,128)}, f32[2,16,512]{2,1,0:T(8,128)}, f32[1,16,512]{2,1,0:T(8,128)}) custom-call(f32[112,512]{1,0:T(8,128)} %shard_map.76.all_ref), custom_call_target="tpu_custom_call" | custom-call | tf_op jit(solution)/shard_map/pallas_call | solution.py:539
